TPU v7x, 32 devices: a whole 2x2x4 slice. The times are simulated.
32 devices in a mesh: ent: 8 (over z, x), qry: 4 (over y, core).
Axes of the slice: x: 2, y: 2, z: 4, core: 2. Of those that a mesh axis runs over, the one named last changes fastest.
Arguments:
- ent_feat: bfloat16 [64, 8192], P(None, 'ent'), may hold values from -6 to 6
- query_head: int32 [16], replicated, may hold values from 0 to 8191
- query_rel: int32 [16], replicated, may hold values from 0 to 821
- query_table: bfloat16 [822, 64], replicated, may hold values from -5 to 5
- rel_table: bfloat16 [3, 822, 64], replicated, may hold values from -5 to 5
- layer_weight: bfloat16 [3, 64, 64], replicated, may hold values from -0.75 to 0.75
- layer_bias: float32 [3, 64], replicated, may hold values from -5 to 5
- norm_gain: float32 [3, 64], replicated, may hold values from 0.5 to 1.5
- norm_shift: float32 [3, 64], replicated, may hold values from -3 to 3
- reg_blocks: int32 [640, 2], P('ent'), may hold values from 0 to 63, as said below
- reg_rel: int32 [640], P('ent'), may hold values from 0 to 821
- reg_mask: int32 [640, 128, 128], P('ent'), may hold values 0 or 1
- hin_blocks: int32 [192, 2], P('ent'), may hold values from 0 to 63, as said below
- hin_rel: int32 [192], P('ent'), may hold values from 0 to 821
- hin_mask: int32 [192, 128, 128], P('ent'), may hold values 0 or 1
- hout_blocks: int32 [192, 2], P('ent'), may hold values from 0 to 63, as said below
- hout_rel: int32 [192], P('ent'), may hold values from 0 to 821
- hout_mask: int32 [192, 128, 128], P('ent'), may hold values 0 or 1
- read_weight: bfloat16 [128, 64], replicated, may hold values from -0.5 to 0.5
- read_bias: float32 [64], replicated, may hold values from -5 to 5
- read_out: float32 [64], replicated, may hold values from -0.75 to 0.75
Outputs:
- scores: float32 [16, 8192], P(None, ('ent', 'qry'))
- hub_scores: float32 [16, 128], P('qry', 'ent')
Inputs may be any that keep to these rules, and one draw needn't show every extreme that they name: `reg_blocks`: rows are grouped by 80 per index of ent. Column 0 is a block of that index's own 8 blocks; column 1 is a block of the same index's or an adjacent index's entities. `hin_blocks`: rows are grouped by 24 per index of ent. Column 0 is a hub block, below 1; column 1 is a block of that index's own entities. `hout_blocks`: rows are grouped by 24 per index of ent. Column 0 is a block of that index's own entities; column 1 is a hub block, below 1.
All inputs are finite; a program needn't handle non-finite values. No bound on the sum of `reg_mask` or of `hin_mask` or of `hout_mask` on one device may be relied on, other than what follows from the above.
Results may differ from a plain program's by a relative error of at most 0.0075.
Values may be sent and summed in bfloat16 or wider, within the bound.
No kernel may reach another device: no remote copies, remote signals or barrier semaphores. Data moves between devices by JAX's collectives and lax.ppermute only.
A program may use at most 128 MiB of HBM per device.

v0:
```python
import jax
import jax.numpy as jnp
from jax import lax
from jax.sharding import PartitionSpec as P

LAYERS = 3
HUB_DEV = 16


def padded(cells, sides, width):
    for axis, dim in sides:
        count = lax.axis_size(axis)
        ends = count - 1
        head = lax.slice_in_dim(cells, 0, width, axis=dim)
        tail = lax.slice_in_dim(cells, cells.shape[dim] - width, cells.shape[dim], axis=dim)
        cells = jnp.concatenate(
            [
                lax.ppermute(tail, axis, [(i, (i + 1) % count) for i in range(ends)]),
                cells,
                lax.ppermute(head, axis, [((i + 1) % count, i) for i in range(ends)]),
            ],
            axis=dim,
        )
    return cells


def normalize(values, along_axis, gain_rows, shift_rows):
    average = jnp.mean(values, axis=along_axis, keepdims=True)
    centered = values - average
    variance = jnp.mean(centered * centered, axis=along_axis, keepdims=True)
    return centered * lax.rsqrt(variance + 1e-05) * gain_rows + shift_rows


def update_hubs(hub_sum, hub_old, weight, bias_row, gain_row, shift_row, q_local, model_width):
    count = hub_sum.shape[0]
    inputs_now = hub_sum.astype(jnp.bfloat16).reshape(count, q_local, model_width)
    linear = (
        jnp.einsum("hqd,de->hqe", inputs_now, weight, preferred_element_type=jnp.float32)
        + bias_row[None, None, :]
    )
    normed = normalize(linear, 2, gain_row[None, None, :], shift_row[None, None, :])
    updated = jax.nn.relu(normed) + hub_old.astype(jnp.float32).reshape(count, q_local, model_width)
    return updated.astype(jnp.bfloat16).reshape(count, q_local * model_width)


def body(
    ent_feat,
    query_head,
    query_rel,
    query_table,
    rel_table,
    layer_weight,
    layer_bias,
    norm_gain,
    norm_shift,
    reg_blocks,
    reg_rel,
    reg_mask,
    hin_blocks,
    hin_rel,
    hin_mask,
    hout_blocks,
    hout_rel,
    hout_mask,
    read_weight,
    read_bias,
    read_out,
):
    ent_devices = lax.axis_size("ent")
    queries = query_head.shape[0]
    q_local = queries // lax.axis_size("qry")
    model_width = ent_feat.shape[0]
    ent_local = ent_feat.shape[1]
    block_size = reg_mask.shape[1]
    blocks_local = ent_local // block_size
    hub_total = HUB_DEV * ent_devices
    hub_block_count = hub_total // block_size
    state_rows = q_local * model_width
    first_block = lax.axis_index("ent") * blocks_local
    first_entity = lax.axis_index("ent") * ent_local
    query_first = lax.axis_index("qry") * q_local
    highest = lax.Precision.HIGHEST
    rel_iota = jnp.arange(query_table.shape[0], dtype=jnp.int32)
    query_onehot = (query_rel[:, None] == rel_iota[None, :]).astype(jnp.bfloat16)
    query_all = jnp.dot(query_onehot, query_table, preferred_element_type=jnp.float32)
    query_local = lax.dynamic_slice_in_dim(query_all, query_first, q_local, 0)
    heads_local = lax.dynamic_slice_in_dim(query_head, query_first, q_local, 0)
    positions = first_entity + jnp.arange(ent_local, dtype=jnp.int32)
    head_hits = (heads_local[:, None] == positions[None, :]).astype(jnp.float32)
    boundary = query_local[:, :, None] * head_hits[:, None, :]
    states = (ent_feat.astype(jnp.float32)[None] + boundary).astype(jnp.bfloat16)
    reg_masks = reg_mask.astype(jnp.bfloat16)
    hin_masks = hin_mask.astype(jnp.bfloat16)
    hout_masks = hout_mask.astype(jnp.bfloat16)
    local_iota = jnp.arange(blocks_local, dtype=jnp.int32)[None, :]
    reg_onehot = (reg_blocks[:, 0][:, None] - first_block == local_iota).astype(jnp.float32)
    reg_sources = reg_blocks[:, 1] - first_block + blocks_local
    hout_onehot = (hout_blocks[:, 0][:, None] - first_block == local_iota).astype(jnp.float32)
    hout_sources = hout_blocks[:, 1]
    hin_onehot = (
        hin_blocks[:, 0][:, None] == jnp.arange(hub_block_count, dtype=jnp.int32)[None, :]
    ).astype(jnp.float32)
    hin_sources = hin_blocks[:, 1] - first_block

    def tile_coefficients(rel_ids, rel_layer):
        rel_onehot = (rel_ids[:, None] == rel_iota[None, :]).astype(jnp.bfloat16)
        rel_rows = jnp.dot(rel_onehot, rel_layer, preferred_element_type=jnp.float32)
        return (query_local[:, :, None] * rel_rows.T[None, :, :]).reshape(state_rows, -1)

    hub_own = jnp.zeros((HUB_DEV, state_rows), jnp.bfloat16)
    for layer_at in range(LAYERS):
        weight = layer_weight[layer_at]
        rel_layer = rel_table[layer_at]
        flat_states = states.reshape(state_rows, ent_local)
        window = padded(flat_states, (("ent", 1),), ent_local)
        window_blocks = window.reshape(state_rows, 3 * blocks_local, block_size)
        gathered = jnp.take(window_blocks, reg_sources, axis=1)
        product = jnp.einsum(
            "ctj,tjk->ctk", gathered, reg_masks, preferred_element_type=jnp.float32
        )
        product = product * tile_coefficients(reg_rel, rel_layer)[:, :, None]
        totals = jnp.einsum("ctk,tb->cbk", product, reg_onehot, precision=highest)
        if layer_at > 0:
            hub_full = lax.all_gather(hub_own, "ent", axis=0, tiled=True)
        else:
            hub_full = jnp.zeros((hub_total, state_rows), jnp.bfloat16)
        hub_view = hub_full.reshape(hub_block_count, block_size, state_rows)
        hub_sources = jnp.take(hub_view, hout_sources, axis=0)
        product = jnp.einsum(
            "tjc,tjk->ctk", hub_sources, hout_masks, preferred_element_type=jnp.float32
        )
        product = product * tile_coefficients(hout_rel, rel_layer)[:, :, None]
        totals = totals + jnp.einsum("ctk,tb->cbk", product, hout_onehot, precision=highest)
        own_blocks = flat_states.reshape(state_rows, blocks_local, block_size)
        hin_gathered = jnp.take(own_blocks, hin_sources, axis=1)
        hin_product = jnp.einsum(
            "ctj,tjk->tkc", hin_gathered, hin_masks, preferred_element_type=jnp.float32
        )
        hin_product = hin_product * tile_coefficients(hin_rel, rel_layer).T[:, None, :]
        partial_value = jnp.einsum(
            "tkc,th->hkc", hin_product, hin_onehot, precision=highest
        ).reshape(hub_total, state_rows)
        inputs_now = (totals.reshape(q_local, model_width, ent_local) + boundary).astype(
            jnp.bfloat16
        )
        linear = (
            jnp.einsum("qdv,de->qev", inputs_now, weight, preferred_element_type=jnp.float32)
            + layer_bias[layer_at][None, :, None]
        )
        normed = normalize(
            linear, 1, norm_gain[layer_at][None, :, None], norm_shift[layer_at][None, :, None]
        )
        states = (jax.nn.relu(normed) + states.astype(jnp.float32)).astype(jnp.bfloat16)
        hub_sum = lax.psum_scatter(partial_value, "ent", scatter_dimension=0, tiled=True)
        hub_own = update_hubs(
            hub_sum,
            hub_own,
            weight,
            layer_bias[layer_at],
            norm_gain[layer_at],
            norm_shift[layer_at],
            q_local,
            model_width,
        )
    read_states = read_weight[:model_width]
    query_part_all = (
        jnp.dot(
            query_all.astype(jnp.bfloat16),
            read_weight[model_width:],
            preferred_element_type=jnp.float32,
        )
        + read_bias[None, :]
    )
    query_part_local = lax.dynamic_slice_in_dim(query_part_all, query_first, q_local, 0)
    moved_states = lax.all_to_all(states, "qry", split_axis=2, concat_axis=0, tiled=True)
    features = jax.nn.relu(
        jnp.einsum("qdv,de->qev", moved_states, read_states, preferred_element_type=jnp.float32)
        + query_part_all[:, :, None]
    )
    scores = jnp.einsum("qev,e->qv", features, read_out, precision=highest)
    hub_view_own = hub_own.reshape(HUB_DEV, q_local, model_width)
    hub_features = jax.nn.relu(
        jnp.einsum("hqd,de->hqe", hub_view_own, read_states, preferred_element_type=jnp.float32)
        + query_part_local[None]
    )
    hub_scores = jnp.einsum("hqe,e->qh", hub_features, read_out, precision=highest)
    return (scores, hub_scores)


def solution(mesh):
    return jax.shard_map(
        body,
        mesh=mesh,
        in_specs=(
            P(None, "ent"),
            P(),
            P(),
            P(),
            P(),
            P(),
            P(),
            P(),
            P(),
            P("ent", None),
            P("ent"),
            P("ent", None, None),
            P("ent", None),
            P("ent"),
            P("ent", None, None),
            P("ent", None),
            P("ent"),
            P("ent", None, None),
            P(),
            P(),
            P(),
        ),
        out_specs=(P(None, ("ent", "qry")), P("qry", "ent")),
        check_vma=False,
    )
```

profile of v0, /device:TPU:0, one launch (start us, length us, event | category | flops | bytes accessed | tf_op | source)
XLA Modules:
  0.0 461.3 jit_solution(1653198230750983543)
XLA Ops:
  12.1 1.3 collective-permute-start.1
  13.4 6.3 %collective-permute-start = (bf16[256,1024]{1,0:T(8,128)(2,1)}, bf16[256,1024]{1,0:T(8,128)(2,1)}, u32[]{:S(2)}, u32[]{:S(2)}) collective-permute-start(bf16[256,1024]{1,0:T(8,128)(2,1)} %fusion.90), channel_id=1, source_target_pairs={{0,4},{4,8},{8,12},{12,16},{16,20},{20,24},{24,28},{1,5},{5,9},{9,... | collective-permute-start | bytes 1572872 | tf_op jit(solution)/shard_map/ppermute | solution.py:18
  21.9 1.1 convolution_bitcast_fusion.5
  23.0 1.1 convolution_bitcast_fusion.6
  27.7 1.2 copy.242
  31.9 1.7 fusion.88
  34.5 2.0 gather_fusion.2
  36.5 1.4 multiply_bitcast_fusion.3
  37.9 4.0 multiply_bitcast_fusion.2
  41.9 3.6 copy.219
  45.5 3.2 fusion.172
  50.2 1.2 convolution_bitcast_fusion
  51.4 1.2 convolution_bitcast_fusion.1
  52.5 1.2 convolution_bitcast_fusion.2
  54.8 1.2 bitcast_multiply_fusion.5
  56.1 3.9 fusion.28
  64.0 48.3 %reduce-scatter.4.cloned.1.call-done = f32[16,256]{1,0:T(8,128)} async-done(((f32[128,256]{1,0:T(8,128)}), f32[16,256]{1,0:T(8,128)}) %reduce-scatter.4.cloned.1.call-update) | async-done | bytes 16400 | tf_op jit(solution)/shard_map/reduce_scatter | solution.py:154
  114.6 1.1 copy.243
  115.7 1.1 copy.240
  117.5 5.9 %gather_fusion = bf16[80,256,128]{2,1,0:T(8,128)(2,1)} fusion(bf16[256,24,128]{2,0,1:T(8,128)(2,1)S(1)} %copy.179, s32[1024]{0:T(1024)} %pad_clamp_fusion.1), kind=kCustom, calls=%fused_computation.clone | custom fusion | bytes 10486080 | tf_op jit(solution)/shard_map/jit(_take)/gather | solution.py:117
  123.5 6.6 %bitcast_multiply_fusion.2 = f32[256,80,128]{2,0,1:T(8,128)S(1)} fusion(f32[256,80]{0,1:T(8,128)S(1)} %copy-done.19, bf16[80,256,128]{2,1,0:T(8,128)(2,1)} %gather_fusion, pred[80]{0:T(512)(128)(4,1)S(1)} %copy-done.37, s32[80,128,128]{2,1,0:T(8,128)} %param.38), kind=kOutput, calls=%fused_computation.8 | convolution fusion | flops 677642240 | bytes 21053520 | tf_op jit(solution)/shard_map/ctj,tjk->ctk/dot_general | solution.py:118
  130.1 9.4 %fusion.78 = bf16[256,8,128]{2,1,0:T(8,128)(2,1)S(1)} fusion(f32[256,8,128]{2,1,0:T(8,128)S(1)} %get-tuple-element.12, f32[8,256,128]{2,0,1:T(8,128)S(1)} %copy-done.15, f32[256,80,128]{2,0,1:T(8,128)S(1)} %bitcast_multiply_fusion.2, s32[80]{0:T(128)S(1)} %copy-done.43), kind=kOutput, calls=%fused_computation.76 | convolution fusion | flops 252445312 | bytes 13107520 | tf_op jit(solution)/shard_map/ctk,tb->cbk/dot_general | solution.py:122
  141.8 1.1 add_convert_fusion.2
  143.8 2.1 gather_fusion.4
  145.9 4.4 multiply_bitcast_fusion.1
  150.3 3.6 copy.222
  153.9 3.2 fusion.170
  159.3 2.0 copy.184
  161.3 1.3 collective-permute-start.3
  162.6 5.4 %collective-permute-start.2 = (bf16[256,1024]{0,1:T(8,128)(2,1)}, bf16[256,1024]{0,1:T(8,128)(2,1)}, u32[]{:S(2)}, u32[]{:S(2)}) collective-permute-start(bf16[256,1024]{0,1:T(8,128)(2,1)} %copy.184), channel_id=1, source_target_pairs={{0,4},{4,8},{8,12},{12,16},{16,20},{20,24},{24,28},{1,5},{5,9},{9,... | collective-permute-start | bytes 1572872 | tf_op jit(solution)/shard_map/ppermute | solution.py:18
  168.0 52.6 %reduce-scatter.6.cloned.1.call-done = f32[16,256]{1,0:T(8,128)} async-done(((f32[128,256]{1,0:T(8,128)}), f32[16,256]{1,0:T(8,128)}) %reduce-scatter.6.cloned.1.call-update) | async-done | bytes 16400 | tf_op jit(solution)/shard_map/reduce_scatter | solution.py:154
  220.6 1.3 convert_element_type.125
  221.9 1.4 reshape.381
  224.4 1.4 add_convert_fusion.5
  226.0 32.4 %all_gather.6 = bf16[128,256]{1,0:T(8,128)(2,1)} all-gather(bf16[16,256]{1,0:T(8,128)(2,1)S(1)} %reshape.378), channel_id=1, replica_groups=mesh['ent'=8,'qry'=4] {'ent'}, dimensions={0}, use_global_device_ids=true | all-gather | bytes 73728 | tf_op jit(solution)/shard_map/all_gather | solution.py:124
  258.4 1.6 copy.195
  260.7 32.4 %all_gather.7 = bf16[128,256]{1,0:T(8,128)(2,1)} all-gather(bf16[16,256]{1,0:T(8,128)(2,1)S(1)} %reshape.382), channel_id=1, replica_groups=mesh['ent'=8,'qry'=4] {'ent'}, dimensions={0}, use_global_device_ids=true | all-gather | bytes 73728 | tf_op jit(solution)/shard_map/all_gather | solution.py:124
  293.1 1.6 copy.209
  294.7 1.8 bitcast_multiply_fusion.4
  296.5 3.8 fusion.26
  300.4 2.4 bitcast_multiply_fusion.3
  302.8 2.0 copy.188
  304.8 2.0 copy.186
  306.9 1.4 pad_maximum_fusion.1
  308.3 5.9 %gather_fusion.1 = bf16[80,256,128]{2,1,0:T(8,128)(2,1)} fusion(bf16[256,24,128]{2,0,1:T(8,128)(2,1)S(1)} %pad_maximum_fusion.1, s32[1024]{0:T(1024)} %pad_clamp_fusion.1), kind=kCustom, calls=%fused_computation.2.clone | custom fusion | bytes 10486080 | tf_op jit(solution)/shard_map/jit(_take)/gather | solution.py:117
  314.2 6.5 %bitcast_multiply_fusion.1 = f32[256,80,128]{2,0,1:T(8,128)S(1)} fusion(f32[256,80]{0,1:T(8,128)S(1)} %copy-done.18, bf16[80,256,128]{2,1,0:T(8,128)(2,1)} %gather_fusion.1, pred[80]{0:T(512)(128)(4,1)S(1)} %copy-done.38, s32[80,128,128]{2,1,0:T(8,128)} %param.38), kind=kOutput, calls=%fused_computation.7 | convolution fusion | flops 677642240 | bytes 21053520 | tf_op jit(solution)/shard_map/ctj,tjk->ctk/dot_general | solution.py:118
  320.8 9.4 %fusion.81 = bf16[256,8,128]{2,1,0:T(8,128)(2,1)S(1)} fusion(f32[256,8,128]{2,1,0:T(8,128)S(1)} %get-tuple-element.12, f32[8,256,128]{2,0,1:T(8,128)S(1)} %copy-done.17, f32[256,80,128]{2,0,1:T(8,128)S(1)} %bitcast_multiply_fusion.1, s32[80]{0:T(128)S(1)} %copy-done.44), kind=kOutput, calls=%fused_computation.77 | convolution fusion | flops 252445312 | bytes 13107520 | tf_op jit(solution)/shard_map/ctk,tb->cbk/dot_general | solution.py:122
  330.4 1.1 fusion.199
  331.8 1.4 add_convert_fusion.1
  334.1 2.1 gather_fusion.5
  336.2 4.2 multiply_bitcast_fusion
  340.4 3.6 copy.226
  343.9 3.2 fusion.168
  347.8 5.7 %fusion.24 = f32[8,256,128]{2,0,1:T(8,128)} fusion(f32[256,24,128]{2,0,1:T(8,128)} %bitcast_multiply_fusion.3, s32[24]{0:T(128)S(1)} %copy-done.48), kind=kOutput, calls=%fused_computation.30 | convolution fusion | flops 75497664 | bytes 4194400 | tf_op jit(solution)/shard_map/ctk,tb->cbk/dot_general | solution.py:133
  353.7 1.3 collective-permute-start.5
  355.0 4.6 collective-permute-start.4
  359.6 49.5 %reduce-scatter.8.cloned.1.call-done = f32[16,256]{1,0:T(8,128)} async-done(((f32[128,256]{1,0:T(8,128)}), f32[16,256]{1,0:T(8,128)}) %reduce-scatter.8.cloned.1.call-update) | async-done | bytes 16400 | tf_op jit(solution)/shard_map/reduce_scatter | solution.py:154
  412.3 1.4 pad_maximum_fusion.2
  413.7 5.8 %gather_fusion.3 = bf16[80,256,128]{2,1,0:T(8,128)(2,1)} fusion(bf16[256,24,128]{2,0,1:T(8,128)(2,1)S(1)} %pad_maximum_fusion.2, s32[1024]{0:T(1024)} %pad_clamp_fusion.1), kind=kCustom, calls=%fused_computation.3.clone | custom fusion | bytes 10486080 | tf_op jit(solution)/shard_map/jit(_take)/gather | solution.py:117
  419.5 6.6 %bitcast_multiply_fusion = f32[256,80,128]{2,0,1:T(8,128)S(1)} fusion(f32[256,80]{0,1:T(8,128)S(1)} %copy.203, bf16[80,256,128]{2,1,0:T(8,128)(2,1)} %gather_fusion.3, pred[80]{0:T(512)(128)(4,1)S(1)} %copy-done.38, s32[80,128,128]{2,1,0:T(8,128)} %param.38), kind=kOutput, calls=%fused_computation.6 | convolution fusion | flops 677642240 | bytes 21053520 | tf_op jit(solution)/shard_map/ctj,tjk->ctk/dot_general | solution.py:118
  426.1 9.4 %fusion.84 = bf16[256,8,128]{2,1,0:T(8,128)(2,1)S(1)} fusion(f32[256,8,128]{2,1,0:T(8,128)S(1)} %get-tuple-element.12, f32[8,256,128]{2,0,1:T(8,128)S(1)} %copy-done.16, f32[256,80,128]{2,0,1:T(8,128)S(1)} %bitcast_multiply_fusion, s32[80]{0:T(128)S(1)} %copy-done.45), kind=kOutput, calls=%fused_computation.78 | convolution fusion | flops 252445312 | bytes 13107520 | tf_op jit(solution)/shard_map/ctk,tb->cbk/dot_general | solution.py:122
  437.7 1.5 reshape.477
  439.2 3.5 all-to-all-start
  443.9 7.6 %all-to-all-done = bf16[4,2,32768]{2,1,0:T(2,128)(2,1)S(1)} async-done(((bf16[4,2,32768]{2,1,0:T(2,128)(2,1)}), bf16[4,2,32768]{2,1,0:T(2,128)(2,1)S(1)}, u32[]{:S(2)}, u32[]{:S(2)}) %all-to-all-start) | async-done | bytes 524320 | tf_op jit(solution)/shard_map/all_to_all | solution.py:175
  (238 shorter events, 42.7 us)
Async XLA Ops:
  7.2 105.1 %reduce-scatter.4.cloned.1.call-start = ((), (), s32[]{:S(2)}) async-start(), calls=%async_computation.4 | async-start | bytes 147456 | tf_op jit(solution)/shard_map/reduce_scatter | solution.py:154
  12.1 102.5 %collective-permute-start.1 = (bf16[256,1024]{1,0:T(8,128)(2,1)}, bf16[256,1024]{1,0:T(8,128)(2,1)}, u32[]{:S(2)}, u32[]{:S(2)}) collective-permute-start(bf16[256,1024]{1,0:T(8,128)(2,1)} %fusion.90), channel_id=1, source_target_pairs={{4,0},{8,4},{12,8},{16,12},{20,16},{24,20},{28,24},{5,1},{9,5},{13... | collective-permute-start | bytes 1572872 | tf_op jit(solution)/shard_map/ppermute | solution.py:20
  13.4 102.4 %collective-permute-start = (bf16[256,1024]{1,0:T(8,128)(2,1)}, bf16[256,1024]{1,0:T(8,128)(2,1)}, u32[]{:S(2)}, u32[]{:S(2)}) collective-permute-start(bf16[256,1024]{1,0:T(8,128)(2,1)} %fusion.90), channel_id=1, source_target_pairs={{0,4},{4,8},{8,12},{12,16},{16,20},{20,24},{24,28},{1,5},{5,9},{9,... | collective-permute-start | bytes 1572872 | tf_op jit(solution)/shard_map/ppermute | solution.py:18
  27.4 4.0 copy-start.35
  31.9 2.6 copy-start.42
  33.6 4.3 copy-start.6
  45.5 4.2 copy-start.62
  45.5 4.7 %copy-start.63 = (s32[80]{0:T(128)S(1)}, s32[80]{0:T(128)}, u32[]{:S(2)}) copy-start(s32[80]{0:T(128)} %param.37) | copy-start | bytes 964
  45.5 8.2 %copy-start.57 = (f32[3,64]{1,0:T(4,128)S(1)}, f32[3,64]{1,0:T(4,128)}, u32[]{:S(2)}) copy-start(f32[3,64]{1,0:T(4,128)} %param.33) | copy-start | bytes 2308
  45.5 8.8 %copy-start.61 = (s32[80,2]{0,1:T(2,128)S(1)}, s32[80,2]{0,1:T(2,128)}, u32[]{:S(2)}) copy-start(s32[80,2]{0,1:T(2,128)} %param.36) | copy-start | bytes 1924
  45.5 9.2 %copy-start.4 = (s32[24,128,128]{2,1,0:T(8,128)S(1)}, s32[24,128,128]{2,1,0:T(8,128)}, u32[]{:S(2)}) copy-start(s32[24,128,128]{2,1,0:T(8,128)} %param.44) | copy-start | bytes 4718596
  49.4 171.2 %reduce-scatter.6.cloned.1.call-start = ((), (), s32[]{:S(2)}) async-start(), calls=%async_computation.5 | async-start | bytes 147456 | tf_op jit(solution)/shard_map/reduce_scatter | solution.py:154
  50.2 9.7 %copy-start.46 = (s32[24]{0:T(128)}, s32[24]{0:T(128)S(1)}, u32[]{:S(2)}) copy-start(s32[24]{0:T(128)S(1)} %subtract_bitcast_fusion) | copy-start | bytes 292
  54.3 58.8 %copy-start.50 = (f32[64]{0:T(128)}, f32[64]{0:T(128)S(1)}, u32[]{:S(2)}) copy-start(f32[64]{0:T(128)S(1)} %get-tuple-element.22) | copy-start | bytes 772
  56.0 3.9 copy-start.58
  56.0 3.9 copy-start.59
  56.0 4.5 copy-start.26
  56.0 4.5 copy-start.34
  56.0 4.5 copy-start.60
  56.0 60.8 %copy-start.14 = (bf16[256,8,128]{2,1,0:T(8,128)(2,1)S(1)}, bf16[256,8,128]{2,1,0:T(8,128)(2,1)}, u32[]{:S(2)}) copy-start(bf16[256,8,128]{2,1,0:T(8,128)(2,1)} %copy-done.13) | copy-start | bytes 1572868
  60.7 51.6 %copy-start.29 = (f32[16,64]{1,0:T(8,128)}, f32[16,64]{1,0:T(8,128)S(1)}, u32[]{:S(2)}) copy-start(f32[16,64]{1,0:T(8,128)S(1)} %convolution_add_fusion.8) | copy-start | bytes 12292
  117.5 6.0 %copy-start.19 = (f32[256,80]{0,1:T(8,128)S(1)}, f32[256,80]{0,1:T(8,128)}, u32[]{:S(2)}) copy-start(f32[256,80]{0,1:T(8,128)} %copy.180) | copy-start | bytes 245764
  117.5 5.9 %copy-start.37 = (pred[80]{0:T(512)(128)(4,1)S(1)}, pred[80]{0:T(512)(128)(4,1)}, u32[]{:S(2)}) copy-start(pred[80]{0:T(512)(128)(4,1)} %get-tuple-element.9) | copy-start | bytes 244
  123.5 6.7 %copy-start.15 = (f32[8,256,128]{2,0,1:T(8,128)S(1)}, f32[8,256,128]{2,0,1:T(8,128)}, u32[]{:S(2)}) copy-start(f32[8,256,128]{2,0,1:T(8,128)} %fusion.28) | copy-start | bytes 3145732
  123.5 6.7 %copy-start.43 = (s32[80]{0:T(128)S(1)}, s32[80]{0:T(128)}, u32[]{:S(2)}) copy-start(s32[80]{0:T(128)} %subtract_bitcast_fusion.1) | copy-start | bytes 964
  130.1 9.6 %copy-start.51 = (f32[64]{0:T(128)S(1)}, f32[64]{0:T(128)}, u32[]{:S(2)}) copy-start(f32[64]{0:T(128)} %copy-done.50) | copy-start | bytes 772
  141.0 2.0 copy-start.22
  141.8 4.1 copy-start.7
  153.9 140.8 %copy-start.5 = (s32[24,128,128]{2,1,0:T(8,128)S(1)}, s32[24,128,128]{2,1,0:T(8,128)}, u32[]{:S(2)}) copy-start(s32[24,128,128]{2,1,0:T(8,128)} %param.44) | copy-start | bytes 4718596
  157.8 251.2 %reduce-scatter.8.cloned.1.call-start = ((), (), s32[]{:S(2)}) async-start(), calls=%async_computation.6 | async-start | bytes 147456 | tf_op jit(solution)/shard_map/reduce_scatter | solution.py:154
  161.3 141.4 %collective-permute-start.3 = (bf16[256,1024]{0,1:T(8,128)(2,1)}, bf16[256,1024]{0,1:T(8,128)(2,1)}, u32[]{:S(2)}, u32[]{:S(2)}) collective-permute-start(bf16[256,1024]{0,1:T(8,128)(2,1)} %copy.184), channel_id=1, source_target_pairs={{4,0},{8,4},{12,8},{16,12},{20,16},{24,20},{28,24},{5,1},{9,5},{13... | collective-permute-start | bytes 1572872 | tf_op jit(solution)/shard_map/ppermute | solution.py:20
  162.6 142.2 %collective-permute-start.2 = (bf16[256,1024]{0,1:T(8,128)(2,1)}, bf16[256,1024]{0,1:T(8,128)(2,1)}, u32[]{:S(2)}, u32[]{:S(2)}) collective-permute-start(bf16[256,1024]{0,1:T(8,128)(2,1)} %copy.184), channel_id=1, source_target_pairs={{0,4},{4,8},{8,12},{12,16},{16,20},{20,24},{24,28},{1,5},{5,9},{9,... | collective-permute-start | bytes 1572872 | tf_op jit(solution)/shard_map/ppermute | solution.py:18
  225.9 70.6 %copy-start.47 = (s32[24]{0:T(128)S(1)}, s32[24]{0:T(128)}, u32[]{:S(2)}) copy-start(s32[24]{0:T(128)} %copy-done.46) | copy-start | bytes 292
  296.5 3.9 copy-start.20
  296.5 3.9 copy-start.25
  296.5 3.8 copy-start.53
  308.2 6.0 %copy-start.18 = (f32[256,80]{0,1:T(8,128)S(1)}, f32[256,80]{0,1:T(8,128)}, u32[]{:S(2)}) copy-start(f32[256,80]{0,1:T(8,128)} %copy.189) | copy-start | bytes 245764
  308.2 5.9 %copy-start.38 = (pred[80]{0:T(512)(128)(4,1)S(1)}, pred[80]{0:T(512)(128)(4,1)}, u32[]{:S(2)}) copy-start(pred[80]{0:T(512)(128)(4,1)} %get-tuple-element.9) | copy-start | bytes 244
  314.2 6.6 %copy-start.17 = (f32[8,256,128]{2,0,1:T(8,128)S(1)}, f32[8,256,128]{2,0,1:T(8,128)}, u32[]{:S(2)}) copy-start(f32[8,256,128]{2,0,1:T(8,128)} %fusion.26) | copy-start | bytes 3145732
  314.2 6.6 %copy-start.44 = (s32[80]{0:T(128)S(1)}, s32[80]{0:T(128)}, u32[]{:S(2)}) copy-start(s32[80]{0:T(128)} %subtract_bitcast_fusion.1) | copy-start | bytes 964
  330.2 1.6 copy-start.3
  330.2 1.6 copy-start.23
  330.2 1.6 copy-start.32
  330.2 1.6 copy-start.40
  330.2 1.6 copy-start.41
  333.2 3.0 copy-start.8
  333.2 2.9 copy-start.24
  333.2 2.9 copy-start.39
  340.4 3.6 copy-start.36
  343.9 3.9 copy-start.48
  343.9 9.5 %copy-start.10 = (bf16[4,64,1024]{2,1,0:T(8,128)(2,1)S(1)}, bf16[4,64,1024]{2,1,0:T(8,128)(2,1)}, u32[]{:S(2)}) copy-start(bf16[4,64,1024]{2,1,0:T(8,128)(2,1)} %copy-done.9) | copy-start | bytes 1572868
  347.1 62.8 %copy-start.21 = (bf16[3,64,64]{2,1,0:T(8,128)(2,1)S(1)}, bf16[3,64,64]{2,1,0:T(8,128)(2,1)}, u32[]{:S(2)}) copy-start(bf16[3,64,64]{2,1,0:T(8,128)(2,1)} %param.32) | copy-start | bytes 73732
  347.1 62.8 %copy-start.49 = (f32[64]{0:T(128)S(1)}, f32[64]{0:T(128)}, u32[]{:S(2)}) copy-start(f32[64]{0:T(128)} %get-tuple-element.21) | copy-start | bytes 772
  353.7 56.6 %collective-permute-start.5 = (bf16[256,1024]{0,1:T(8,128)(2,1)S(1)}, bf16[256,1024]{0,1:T(8,128)(2,1)S(1)}, u32[]{:S(2)}, u32[]{:S(2)}) collective-permute-start(bf16[256,1024]{0,1:T(8,128)(2,1)S(1)} %copy.198), channel_id=1, source_target_pairs={{4,0},{8,4},{12,8},{16,12},{20,16},{24,20},{28,24},{5,1},{9,5},{13... | collective-permute-start | bytes 1572872 | tf_op jit(solution)/shard_map/ppermute | solution.py:20
  355.0 56.3 %collective-permute-start.4 = (bf16[256,1024]{0,1:T(8,128)(2,1)S(1)}, bf16[256,1024]{0,1:T(8,128)(2,1)S(1)}, u32[]{:S(2)}, u32[]{:S(2)}) collective-permute-start(bf16[256,1024]{0,1:T(8,128)(2,1)S(1)} %copy.198), channel_id=1, source_target_pairs={{0,4},{4,8},{8,12},{12,16},{16,20},{20,24},{24,28},{1,5},{5,9},{9,... | collective-permute-start | bytes 1572872 | tf_op jit(solution)/shard_map/ppermute | solution.py:18
  419.5 6.6 %copy-start.16 = (f32[8,256,128]{2,0,1:T(8,128)S(1)}, f32[8,256,128]{2,0,1:T(8,128)}, u32[]{:S(2)}) copy-start(f32[8,256,128]{2,0,1:T(8,128)} %fusion.24) | copy-start | bytes 3145732
  419.5 6.6 %copy-start.45 = (s32[80]{0:T(128)S(1)}, s32[80]{0:T(128)}, u32[]{:S(2)}) copy-start(s32[80]{0:T(128)} %subtract_bitcast_fusion.1) | copy-start | bytes 964
  436.6 6.1 %copy-start.27 = (bf16[128,64]{0,1:T(8,128)(2,1)S(1)}, bf16[128,64]{0,1:T(8,128)(2,1)}, u32[]{:S(2)}) copy-start(bf16[128,64]{0,1:T(8,128)(2,1)} %param.45) | copy-start | bytes 49156
  436.6 6.1 %copy-start.28 = (bf16[16,4,64]{2,0,1:T(8,128)(2,1)S(1)}, bf16[16,4,64]{2,0,1:T(8,128)(2,1)}, u32[]{:S(2)}) copy-start(bf16[16,4,64]{2,0,1:T(8,128)(2,1)} %get-tuple-element.4) | copy-start | bytes 24580
  436.6 6.1 %copy-start.54 = (f32[4,64]{1,0:T(4,128)S(1)}, f32[4,64]{1,0:T(4,128)}, u32[]{:S(2)}) copy-start(f32[4,64]{1,0:T(4,128)} %constant_dynamic-slice_fusion) | copy-start | bytes 3076
  436.6 6.4 %copy-start.52 = (f32[64]{0:T(128)S(1)}, f32[64]{0:T(128)}, u32[]{:S(2)}) copy-start(f32[64]{0:T(128)} %param.47) | copy-start | bytes 772
  437.6 15.1 %copy-start.30 = (f32[16,64]{1,0:T(8,128)S(1)}, f32[16,64]{1,0:T(8,128)}, u32[]{:S(2)}) copy-start(f32[16,64]{1,0:T(8,128)} %copy-done.29) | copy-start | bytes 12292
  439.2 12.3 %all-to-all-start = ((bf16[4,2,32768]{2,1,0:T(2,128)(2,1)}), bf16[4,2,32768]{2,1,0:T(2,128)(2,1)S(1)}, u32[]{:S(2)}, u32[]{:S(2)}) async-start(bf16[4,2,32768]{2,1,0:T(2,128)(2,1)} %reshape.477), calls=%async_computation.2 | async-start | bytes 1048576 | tf_op jit(solution)/shard_map/all_to_all | solution.py:175
  442.7 11.6 %copy-start.1 = (bf16[822,64]{0,1:T(8,128)(2,1)S(1)}, bf16[822,64]{0,1:T(8,128)(2,1)}, u32[]{:S(2)}) copy-start(bf16[822,64]{0,1:T(8,128)(2,1)} %param.30) | copy-start | bytes 315652
  (10 other events, 8.6 us)
Sparse Core Ops, SparseCore 0:
  49.6 62.6 reduce-scatter.3
  158.0 62.5 reduce-scatter.5
  347.9 61.0 reduce-scatter.7
where the time goes:
time: 468 us; the launch traced here: 461 us
  waiting for transfers between devices  158 us (34%)
  matrix products  107 us (23%)
  local copies, waits for them, and re-layouts  71.9 us (15%)
  blocking collectives  64.8 us (14%)
  starting transfers between devices  23.9 us (5%)
  other arithmetic  20.6 us (4%)
  between operations  15.3 us (3%)
    reduce_scatter x3, waiting for transfers between devices, body(): lax.psum_scatter(partial_value, 'ent', scatter_dimension=0, tiled=True)  150 us
    all_gather x2, blocking collectives, body(): hub_full = lax.all_gather(hub_own, 'ent', axis=0, tiled=True)  64.8 us
    dot_general x3, matrix products, body(): totals = jnp.einsum('ctk,tb->cbk', product, reg_onehot, precision=highest)  28.1 us
    dot_general x3, matrix products, body(): jnp.einsum('ctj,tjk->ctk', gathered, reg_masks, preferred_element_type=jn...  19.8 us
    gather x3, local copies, waits for them, and re-layouts, body(): gathered = jnp.take(window_blocks, reg_sources, axis=1)  17.7 us
    ppermute x3, starting transfers between devices, padded(): lax.ppermute(tail, axis, [(i, (i + 1) % count) for i in range(ends)])  16.3 us
    dot_general x3, matrix products, body(): jnp.einsum('ctk,tb->cbk', product, hout_onehot, precision=highest)  13.3 us
    dot_general x3, matrix products, body(): jnp.einsum('ctj,tjk->tkc', hin_gathered, hin_masks, preferred_element_typ...  12.6 us
  transfers between devices with their start and end apart: 10, of which 4 were waited for; matrix products, arithmetic and copies ran while one was open for 17% of the time, Pallas kernels for 0%

commit v1 on v0

--- a/solution.py
+++ b/solution.py
@@ -121,7 +121,11 @@
         product = product * tile_coefficients(reg_rel, rel_layer)[:, :, None]
         totals = jnp.einsum("ctk,tb->cbk", product, reg_onehot, precision=highest)
         if layer_at > 0:
-            hub_full = lax.all_gather(hub_own, "ent", axis=0, tiled=True)
+            peers = lax.axis_size("ent")
+            repeats = [peers if d == 0 else 1 for d in range(hub_own.ndim)]
+            hub_full = lax.all_to_all(
+                jnp.tile(hub_own, repeats), "ent", split_axis=0, concat_axis=0, tiled=True
+            )
         else:
             hub_full = jnp.zeros((hub_total, state_rows), jnp.bfloat16)
         hub_view = hub_full.reshape(hub_block_count, block_size, state_rows)

time: 468 us -> 436 us (0.932)
  blocking collectives: 64.8 us -> 0 us
  waiting for transfers between devices: 158 us -> 184 us
  starting transfers between devices: 23.9 us -> 32 us
    all_gather x2 -> x0, blocking collectives: 64.8 us -> none  [body(): hub_full = lax.all_gather(hub_own, 'ent', axis=0, tiled=True)]
    reduce_scatter x3, waiting for transfers between devices: 150 us -> 167 us  [body(): lax.psum_scatter(partial_value, 'ent', scatter_dimension=0, tiled=True)]
    all_to_all x0 -> x2, starting transfers between devices: none -> 7.62 us  [body(): lax.all_to_all(jnp.tile(hub_own, repeats), 'ent', split_axis=0, concat_ax...]
    all_to_all x0 -> x2, waiting for transfers between devices: none -> 6.09 us  [body(): lax.all_to_all(jnp.tile(hub_own, repeats), 'ent', split_axis=0, concat_ax...]
    unnamed x136 -> x134, local copies, waits for them, and re-layouts: 10.7 us -> 10.8 us
  transfers between devices with their start and end apart: 10 -> 12, of which waited for: 4 -> 6; matrix products, arithmetic and copies ran while one was open for 17% -> 17% of each run, Pallas kernels for 0% -> 0%
where the time goes in v1:
time: 436 us; the launch traced here: 429 us
  waiting for transfers between devices  184 us (42%)
  matrix products  104 us (24%)
  local copies, waits for them, and re-layouts  73.6 us (17%)
  starting transfers between devices  32 us (7%)
  other arithmetic  20.2 us (5%)
  between operations  15.2 us (3%)
    reduce_scatter x3, waiting for transfers between devices, body(): lax.psum_scatter(partial_value, 'ent', scatter_dimension=0, tiled=True)  167 us
    dot_general x3, matrix products, body(): totals = jnp.einsum('ctk,tb->cbk', product, reg_onehot, precision=highest)  28.1 us
    dot_general x3, matrix products, body(): jnp.einsum('ctj,tjk->ctk', gathered, reg_masks, preferred_element_type=jn...  19.8 us
    gather x3, local copies, waits for them, and re-layouts, body(): gathered = jnp.take(window_blocks, reg_sources, axis=1)  17.5 us
    ppermute x3, starting transfers between devices, padded(): lax.ppermute(tail, axis, [(i, (i + 1) % count) for i in range(ends)])  16.7 us
    dot_general x3, matrix products, body(): jnp.einsum('ctk,tb->cbk', product, hout_onehot, precision=highest)  13.4 us
    dot_general x3, matrix products, body(): jnp.einsum('ctj,tjk->tkc', hin_gathered, hin_masks, preferred_element_typ...  12.7 us
    unnamed x134, local copies, waits for them, and re-layouts  10.8 us
  transfers between devices with their start and end apart: 12, of which 6 were waited for; matrix products, arithmetic and copies ran while one was open for 17% of the time, Pallas kernels for 0%

profile of v1, /device:TPU:0, one launch (start us, length us, event | category | flops | bytes accessed | tf_op | source)
XLA Modules:
  0.0 429.4 jit_solution(3800619592863717761)
XLA Ops:
  12.1 1.3 collective-permute-start.1
  13.4 6.3 %collective-permute-start = (bf16[256,1024]{1,0:T(8,128)(2,1)}, bf16[256,1024]{1,0:T(8,128)(2,1)}, u32[]{:S(2)}, u32[]{:S(2)}) collective-permute-start(bf16[256,1024]{1,0:T(8,128)(2,1)} %fusion.90), channel_id=1, source_target_pairs={{0,4},{4,8},{8,12},{12,16},{16,20},{20,24},{24,28},{1,5},{5,9},{9,... | collective-permute-start | bytes 1572872 | tf_op jit(solution)/shard_map/ppermute | solution.py:18
  20.8 1.1 convolution_bitcast_fusion.7
  21.9 1.1 convolution_bitcast_fusion.5
  23.0 1.1 convolution_bitcast_fusion.6
  24.1 1.1 convolution_bitcast_fusion.4
  27.7 1.2 copy.242
  32.0 1.7 fusion.88
  34.6 2.0 gather_fusion.2
  36.6 1.4 multiply_bitcast_fusion.3
  38.0 4.0 multiply_bitcast_fusion.2
  42.0 3.6 copy.219
  45.6 3.2 fusion.172
  53.3 1.2 bitcast_multiply_fusion.5
  54.5 3.9 fusion.28
  60.1 52.3 %reduce-scatter.4.cloned.1.call-done = f32[16,256]{1,0:T(8,128)} async-done(((f32[128,256]{1,0:T(8,128)}), f32[16,256]{1,0:T(8,128)}) %reduce-scatter.4.cloned.1.call-update) | async-done | bytes 16400 | tf_op jit(solution)/shard_map/reduce_scatter | solution.py:158
  114.7 1.1 copy.243
  115.8 1.1 copy.240
  117.6 5.8 %gather_fusion = bf16[80,256,128]{2,1,0:T(8,128)(2,1)} fusion(bf16[256,24,128]{2,0,1:T(8,128)(2,1)S(1)} %copy.179, s32[1024]{0:T(1024)} %pad_clamp_fusion.1), kind=kCustom, calls=%fused_computation.clone | custom fusion | bytes 10486080 | tf_op jit(solution)/shard_map/jit(_take)/gather | solution.py:117
  123.4 6.6 %bitcast_multiply_fusion.2 = f32[256,80,128]{2,0,1:T(8,128)S(1)} fusion(f32[256,80]{0,1:T(8,128)S(1)} %copy.180, bf16[80,256,128]{2,1,0:T(8,128)(2,1)} %gather_fusion, pred[80]{0:T(512)(128)(4,1)S(1)} %copy-done.39, s32[80,128,128]{2,1,0:T(8,128)} %param.38), kind=kOutput, calls=%fused_computation.8 | convolution fusion | flops 677642240 | bytes 21053520 | tf_op jit(solution)/shard_map/ctj,tjk->ctk/dot_general | solution.py:118
  130.1 9.4 %fusion.78 = bf16[256,8,128]{2,1,0:T(8,128)(2,1)S(1)} fusion(f32[256,8,128]{2,1,0:T(8,128)S(1)} %get-tuple-element.12, f32[8,256,128]{2,0,1:T(8,128)S(1)} %copy-done.16, f32[256,80,128]{2,0,1:T(8,128)S(1)} %bitcast_multiply_fusion.2, s32[80]{0:T(128)S(1)} %copy-done.42), kind=kOutput, calls=%fused_computation.76 | convolution fusion | flops 252445312 | bytes 13107520 | tf_op jit(solution)/shard_map/ctk,tb->cbk/dot_general | solution.py:122
  141.0 1.1 add_convert_fusion.2
  143.0 2.1 gather_fusion.4
  145.1 4.5 %multiply_bitcast_fusion.1 = f32[24,128,256]{1,2,0:T(8,128)} fusion(bf16[24,256,128]{2,1,0:T(8,128)(2,1)} %gather_fusion.4, f32[24,256]{1,0:T(8,128)} %get-tuple-element.27, pred[24]{0:T(512)(128)(4,1)S(1)} %copy-done.37, s32[24,128,128]{2,1,0:T(8,128)S(1)} %copy-done.7), kind=kOutput, calls=%fused_computation.37 | convolution fusion | flops 203292672 | bytes 6316056 | tf_op jit(solution)/shard_map/ctj,tjk->tkc/dot_general | solution.py:140
  149.6 3.6 copy.222
  153.2 3.2 fusion.170
  157.9 60.3 %reduce-scatter.6.cloned.1.call-done = f32[16,256]{1,0:T(8,128)} async-done(((f32[128,256]{1,0:T(8,128)}), f32[16,256]{1,0:T(8,128)}) %reduce-scatter.6.cloned.1.call-update) | async-done | bytes 16400 | tf_op jit(solution)/shard_map/reduce_scatter | solution.py:158
  220.7 1.4 add_convert_fusion.5
  222.8 3.6 all-to-all-start
  227.3 6.1 %all-to-all-done = bf16[8,16,256]{2,1,0:T(8,128)(2,1)S(1)} async-done(((bf16[8,16,256]{2,1,0:T(8,128)(2,1)}), bf16[8,16,256]{2,1,0:T(8,128)(2,1)S(1)}, u32[]{:S(2)}, u32[]{:S(2)}) %all-to-all-start) | async-done | bytes 65568 | tf_op jit(solution)/shard_map/all_to_all | solution.py:126
  234.0 4.0 all-to-all-start.1
  239.0 1.6 copy.189
  242.2 2.0 copy.184
  244.3 1.3 collective-permute-start.3
  245.5 5.3 %collective-permute-start.2 = (bf16[256,1024]{0,1:T(8,128)(2,1)}, bf16[256,1024]{0,1:T(8,128)(2,1)}, u32[]{:S(2)}, u32[]{:S(2)}) collective-permute-start(bf16[256,1024]{0,1:T(8,128)(2,1)} %copy.184), channel_id=1, source_target_pairs={{0,4},{4,8},{8,12},{12,16},{16,20},{20,24},{24,28},{1,5},{5,9},{9,... | collective-permute-start | bytes 1572872 | tf_op jit(solution)/shard_map/ppermute | solution.py:18
  250.9 1.6 copy.195
  252.5 1.6 copy.209
  254.0 1.8 bitcast_multiply_fusion.4
  255.8 3.8 fusion.26
  259.7 2.4 bitcast_multiply_fusion.3
  262.1 2.0 copy.188
  264.1 3.8 collective-permute-done.2
  268.0 2.0 copy.186
  270.0 1.4 pad_maximum_fusion.1
  271.4 5.9 %gather_fusion.1 = bf16[80,256,128]{2,1,0:T(8,128)(2,1)} fusion(bf16[256,24,128]{2,0,1:T(8,128)(2,1)S(1)} %pad_maximum_fusion.1, s32[1024]{0:T(1024)} %pad_clamp_fusion.1), kind=kCustom, calls=%fused_computation.2.clone | custom fusion | bytes 10486080 | tf_op jit(solution)/shard_map/jit(_take)/gather | solution.py:117
  277.4 6.5 %bitcast_multiply_fusion.1 = f32[256,80,128]{2,0,1:T(8,128)S(1)} fusion(f32[256,80]{0,1:T(8,128)S(1)} %copy-done.18, bf16[80,256,128]{2,1,0:T(8,128)(2,1)} %gather_fusion.1, pred[80]{0:T(512)(128)(4,1)S(1)} %copy-done.40, s32[80,128,128]{2,1,0:T(8,128)} %param.38), kind=kOutput, calls=%fused_computation.7 | convolution fusion | flops 677642240 | bytes 21053520 | tf_op jit(solution)/shard_map/ctj,tjk->ctk/dot_general | solution.py:118
  283.9 9.4 %fusion.81 = bf16[256,8,128]{2,1,0:T(8,128)(2,1)S(1)} fusion(f32[256,8,128]{2,1,0:T(8,128)S(1)} %get-tuple-element.12, f32[8,256,128]{2,0,1:T(8,128)S(1)} %copy-done.17, f32[256,80,128]{2,0,1:T(8,128)S(1)} %bitcast_multiply_fusion.1, s32[80]{0:T(128)S(1)} %copy-done.43), kind=kOutput, calls=%fused_computation.77 | convolution fusion | flops 252445312 | bytes 13107520 | tf_op jit(solution)/shard_map/ctk,tb->cbk/dot_general | solution.py:122
  293.6 1.1 fusion.199
  295.0 1.3 add_convert_fusion.1
  297.2 2.1 gather_fusion.5
  299.3 4.2 multiply_bitcast_fusion
  303.5 3.6 copy.226
  307.1 3.2 fusion.168
  310.9 5.7 %fusion.24 = f32[8,256,128]{2,0,1:T(8,128)} fusion(f32[256,24,128]{2,0,1:T(8,128)} %bitcast_multiply_fusion.3, s32[24]{0:T(128)S(1)} %copy-done.47), kind=kOutput, calls=%fused_computation.30 | convolution fusion | flops 75497664 | bytes 4194400 | tf_op jit(solution)/shard_map/ctk,tb->cbk/dot_general | solution.py:137
  316.8 1.3 collective-permute-start.5
  318.1 5.1 %collective-permute-start.4 = (bf16[256,1024]{0,1:T(8,128)(2,1)S(1)}, bf16[256,1024]{0,1:T(8,128)(2,1)S(1)}, u32[]{:S(2)}, u32[]{:S(2)}) collective-permute-start(bf16[256,1024]{0,1:T(8,128)(2,1)S(1)} %copy.198), channel_id=1, source_target_pairs={{0,4},{4,8},{8,12},{12,16},{16,20},{20,24},{24,28},{1,5},{5,9},{9,... | collective-permute-start | bytes 1572872 | tf_op jit(solution)/shard_map/ppermute | solution.py:18
  323.2 54.0 %reduce-scatter.8.cloned.1.call-done = f32[16,256]{1,0:T(8,128)} async-done(((f32[128,256]{1,0:T(8,128)}), f32[16,256]{1,0:T(8,128)}) %reduce-scatter.8.cloned.1.call-update) | async-done | bytes 16400 | tf_op jit(solution)/shard_map/reduce_scatter | solution.py:158
  380.5 1.4 pad_maximum_fusion.2
  381.8 5.8 %gather_fusion.3 = bf16[80,256,128]{2,1,0:T(8,128)(2,1)} fusion(bf16[256,24,128]{2,0,1:T(8,128)(2,1)S(1)} %pad_maximum_fusion.2, s32[1024]{0:T(1024)} %pad_clamp_fusion.1), kind=kCustom, calls=%fused_computation.3.clone | custom fusion | bytes 10486080 | tf_op jit(solution)/shard_map/jit(_take)/gather | solution.py:117
  387.6 6.6 %bitcast_multiply_fusion = f32[256,80,128]{2,0,1:T(8,128)S(1)} fusion(f32[256,80]{0,1:T(8,128)S(1)} %copy.203, bf16[80,256,128]{2,1,0:T(8,128)(2,1)} %gather_fusion.3, pred[80]{0:T(512)(128)(4,1)S(1)} %copy-done.40, s32[80,128,128]{2,1,0:T(8,128)} %param.38), kind=kOutput, calls=%fused_computation.6 | convolution fusion | flops 677642240 | bytes 21053520 | tf_op jit(solution)/shard_map/ctj,tjk->ctk/dot_general | solution.py:118
  394.3 9.4 %fusion.84 = bf16[256,8,128]{2,1,0:T(8,128)(2,1)S(1)} fusion(f32[256,8,128]{2,1,0:T(8,128)S(1)} %get-tuple-element.12, f32[8,256,128]{2,0,1:T(8,128)S(1)} %copy-done.15, f32[256,80,128]{2,0,1:T(8,128)S(1)} %bitcast_multiply_fusion, s32[80]{0:T(128)S(1)} %copy-done.44), kind=kOutput, calls=%fused_computation.78 | convolution fusion | flops 252445312 | bytes 13107520 | tf_op jit(solution)/shard_map/ctk,tb->cbk/dot_general | solution.py:122
  405.8 1.6 reshape.487
  407.3 3.5 all-to-all-start.2
  412.0 7.6 %all-to-all-done.2 = bf16[4,2,32768]{2,1,0:T(2,128)(2,1)S(1)} async-done(((bf16[4,2,32768]{2,1,0:T(2,128)(2,1)}), bf16[4,2,32768]{2,1,0:T(2,128)(2,1)S(1)}, u32[]{:S(2)}, u32[]{:S(2)}) %all-to-all-start.2) | async-done | bytes 524320 | tf_op jit(solution)/shard_map/all_to_all | solution.py:179
  (240 shorter events, 43.9 us)
Async XLA Ops:
  7.2 105.2 %reduce-scatter.4.cloned.1.call-start = ((), (), s32[]{:S(2)}) async-start(), calls=%async_computation.6 | async-start | bytes 147456 | tf_op jit(solution)/shard_map/reduce_scatter | solution.py:158
  12.1 102.6 %collective-permute-start.1 = (bf16[256,1024]{1,0:T(8,128)(2,1)}, bf16[256,1024]{1,0:T(8,128)(2,1)}, u32[]{:S(2)}, u32[]{:S(2)}) collective-permute-start(bf16[256,1024]{1,0:T(8,128)(2,1)} %fusion.90), channel_id=1, source_target_pairs={{4,0},{8,4},{12,8},{16,12},{20,16},{24,20},{28,24},{5,1},{9,5},{13... | collective-permute-start | bytes 1572872 | tf_op jit(solution)/shard_map/ppermute | solution.py:20
  13.4 102.5 %collective-permute-start = (bf16[256,1024]{1,0:T(8,128)(2,1)}, bf16[256,1024]{1,0:T(8,128)(2,1)}, u32[]{:S(2)}, u32[]{:S(2)}) collective-permute-start(bf16[256,1024]{1,0:T(8,128)(2,1)} %fusion.90), channel_id=1, source_target_pairs={{0,4},{4,8},{8,12},{12,16},{16,20},{20,24},{24,28},{1,5},{5,9},{9,... | collective-permute-start | bytes 1572872 | tf_op jit(solution)/shard_map/ppermute | solution.py:18
  27.4 4.0 copy-start.34
  32.0 2.6 copy-start.41
  32.0 4.6 %copy-start.27 = (f32[256,24]{0,1:T(8,128)S(1)}, f32[256,24]{0,1:T(8,128)}, u32[]{:S(2)}) copy-start(f32[256,24]{0,1:T(8,128)} %mul.455) | copy-start | bytes 73732
  33.7 4.3 %copy-start.6 = (s32[24,128,128]{2,1,0:T(8,128)S(1)}, s32[24,128,128]{2,1,0:T(8,128)}, u32[]{:S(2)}) copy-start(s32[24,128,128]{2,1,0:T(8,128)} %param.41) | copy-start | bytes 4718596
  45.5 4.2 copy-start.61
  45.5 4.8 %copy-start.60 = (bf16[3,822,64]{1,2,0:T(8,128)(2,1)S(1)}, bf16[3,822,64]{1,2,0:T(8,128)(2,1)}, u32[]{:S(2)}) copy-start(bf16[3,822,64]{1,2,0:T(8,128)(2,1)} %param.31) | copy-start | bytes 946948
  45.6 4.8 %copy-start.62 = (s32[80]{0:T(128)S(1)}, s32[80]{0:T(128)}, u32[]{:S(2)}) copy-start(s32[80]{0:T(128)} %param.37) | copy-start | bytes 964
  45.6 5.6 %copy-start.56 = (f32[3,64]{1,0:T(4,128)S(1)}, f32[3,64]{1,0:T(4,128)}, u32[]{:S(2)}) copy-start(f32[3,64]{1,0:T(4,128)} %param.33) | copy-start | bytes 2308
  45.6 7.1 %copy-start.59 = (s32[80,2]{0,1:T(2,128)S(1)}, s32[80,2]{0,1:T(2,128)}, u32[]{:S(2)}) copy-start(s32[80,2]{0,1:T(2,128)} %param.36) | copy-start | bytes 1924
  45.6 7.7 %copy-start.4 = (s32[24,128,128]{2,1,0:T(8,128)S(1)}, s32[24,128,128]{2,1,0:T(8,128)}, u32[]{:S(2)}) copy-start(s32[24,128,128]{2,1,0:T(8,128)} %param.44) | copy-start | bytes 4718596
  49.5 168.6 %reduce-scatter.6.cloned.1.call-start = ((), (), s32[]{:S(2)}) async-start(), calls=%async_computation.7 | async-start | bytes 147456 | tf_op jit(solution)/shard_map/reduce_scatter | solution.py:158
  50.4 8.0 %copy-start.45 = (s32[24]{0:T(128)}, s32[24]{0:T(128)S(1)}, u32[]{:S(2)}) copy-start(s32[24]{0:T(128)S(1)} %subtract_bitcast_fusion) | copy-start | bytes 292
  51.8 61.4 %copy-start.49 = (f32[64]{0:T(128)}, f32[64]{0:T(128)S(1)}, u32[]{:S(2)}) copy-start(f32[64]{0:T(128)S(1)} %get-tuple-element.22) | copy-start | bytes 772
  54.5 3.9 copy-start.57
  54.5 3.9 copy-start.58
  54.5 62.5 %copy-start.14 = (bf16[256,8,128]{2,1,0:T(8,128)(2,1)S(1)}, bf16[256,8,128]{2,1,0:T(8,128)(2,1)}, u32[]{:S(2)}) copy-start(bf16[256,8,128]{2,1,0:T(8,128)(2,1)} %copy-done.13) | copy-start | bytes 1572868
  117.6 5.8 %copy-start.39 = (pred[80]{0:T(512)(128)(4,1)S(1)}, pred[80]{0:T(512)(128)(4,1)}, u32[]{:S(2)}) copy-start(pred[80]{0:T(512)(128)(4,1)} %get-tuple-element.9) | copy-start | bytes 244
  123.4 6.6 %copy-start.16 = (f32[8,256,128]{2,0,1:T(8,128)S(1)}, f32[8,256,128]{2,0,1:T(8,128)}, u32[]{:S(2)}) copy-start(f32[8,256,128]{2,0,1:T(8,128)} %fusion.28) | copy-start | bytes 3145732
  123.4 6.6 %copy-start.42 = (s32[80]{0:T(128)S(1)}, s32[80]{0:T(128)}, u32[]{:S(2)}) copy-start(s32[80]{0:T(128)} %subtract_bitcast_fusion.1) | copy-start | bytes 964
  130.1 9.6 %copy-start.21 = (bf16[3,64,64]{2,1,0:T(8,128)(2,1)S(1)}, bf16[3,64,64]{2,1,0:T(8,128)(2,1)}, u32[]{:S(2)}) copy-start(bf16[3,64,64]{2,1,0:T(8,128)(2,1)} %param.32) | copy-start | bytes 73732
  130.1 9.6 %copy-start.50 = (f32[64]{0:T(128)S(1)}, f32[64]{0:T(128)}, u32[]{:S(2)}) copy-start(f32[64]{0:T(128)} %copy-done.49) | copy-start | bytes 772
  140.3 4.9 %copy-start.23 = (f32[4,1024]{1,0:T(4,128)}, f32[4,1024]{1,0:T(4,128)S(1)}, u32[]{:S(2)}) copy-start(f32[4,1024]{1,0:T(4,128)S(1)} %add_rsqrt_fusion.2) | copy-start | bytes 49156
  141.0 4.1 copy-start.7
  141.0 4.1 copy-start.37
  149.6 3.6 copy-start.35
  153.2 3.9 copy-start.32
  153.2 100.8 %copy-start.5 = (s32[24,128,128]{2,1,0:T(8,128)S(1)}, s32[24,128,128]{2,1,0:T(8,128)}, u32[]{:S(2)}) copy-start(s32[24,128,128]{2,1,0:T(8,128)} %param.44) | copy-start | bytes 4718596
  222.8 10.5 %all-to-all-start = ((bf16[8,16,256]{2,1,0:T(8,128)(2,1)}), bf16[8,16,256]{2,1,0:T(8,128)(2,1)S(1)}, u32[]{:S(2)}, u32[]{:S(2)}) async-start(bf16[8,16,256]{2,1,0:T(8,128)(2,1)} %tile.17), calls=%async_computation.1 | async-start | bytes 131072 | tf_op jit(solution)/shard_map/all_to_all | solution.py:126
  233.4 7.3 %copy-start.20 = (bf16[8,16,256]{2,1,0:T(8,128)(2,1)}, bf16[8,16,256]{2,1,0:T(8,128)(2,1)S(1)}, u32[]{:S(2)}) copy-start(bf16[8,16,256]{2,1,0:T(8,128)(2,1)S(1)} %all-to-all-done) | copy-start | bytes 196612
  234.0 18.4 %all-to-all-start.1 = ((bf16[8,16,256]{2,1,0:T(8,128)(2,1)}), bf16[8,16,256]{2,1,0:T(8,128)(2,1)}, u32[]{:S(2)}, u32[]{:S(2)}) async-start(bf16[8,16,256]{2,1,0:T(8,128)(2,1)} %tile.19), calls=%async_computation.3 | async-start | bytes 131072 | tf_op jit(solution)/shard_map/all_to_all | solution.py:126
  238.0 139.2 %reduce-scatter.8.cloned.1.call-start = ((), (), s32[]{:S(2)}) async-start(), calls=%async_computation.8 | async-start | bytes 147456 | tf_op jit(solution)/shard_map/reduce_scatter | solution.py:158
  240.6 15.2 %copy-start.46 = (s32[24]{0:T(128)S(1)}, s32[24]{0:T(128)}, u32[]{:S(2)}) copy-start(s32[24]{0:T(128)} %copy-done.45) | copy-start | bytes 292
  244.3 17.9 %collective-permute-start.3 = (bf16[256,1024]{0,1:T(8,128)(2,1)}, bf16[256,1024]{0,1:T(8,128)(2,1)}, u32[]{:S(2)}, u32[]{:S(2)}) collective-permute-start(bf16[256,1024]{0,1:T(8,128)(2,1)} %copy.184), channel_id=1, source_target_pairs={{4,0},{8,4},{12,8},{16,12},{20,16},{24,20},{28,24},{5,1},{9,5},{13... | collective-permute-start | bytes 1572872 | tf_op jit(solution)/shard_map/ppermute | solution.py:20
  245.5 22.4 %collective-permute-start.2 = (bf16[256,1024]{0,1:T(8,128)(2,1)}, bf16[256,1024]{0,1:T(8,128)(2,1)}, u32[]{:S(2)}, u32[]{:S(2)}) collective-permute-start(bf16[256,1024]{0,1:T(8,128)(2,1)} %copy.184), channel_id=1, source_target_pairs={{0,4},{4,8},{8,12},{12,16},{16,20},{20,24},{24,28},{1,5},{5,9},{9,... | collective-permute-start | bytes 1572872 | tf_op jit(solution)/shard_map/ppermute | solution.py:18
  255.8 3.9 copy-start.19
  255.8 3.9 copy-start.26
  255.8 3.9 copy-start.52
  271.4 5.9 %copy-start.18 = (f32[256,80]{0,1:T(8,128)S(1)}, f32[256,80]{0,1:T(8,128)}, u32[]{:S(2)}) copy-start(f32[256,80]{0,1:T(8,128)} %copy.189) | copy-start | bytes 245764
  271.4 5.9 %copy-start.40 = (pred[80]{0:T(512)(128)(4,1)S(1)}, pred[80]{0:T(512)(128)(4,1)}, u32[]{:S(2)}) copy-start(pred[80]{0:T(512)(128)(4,1)} %get-tuple-element.9) | copy-start | bytes 244
  277.3 6.6 %copy-start.17 = (f32[8,256,128]{2,0,1:T(8,128)S(1)}, f32[8,256,128]{2,0,1:T(8,128)}, u32[]{:S(2)}) copy-start(f32[8,256,128]{2,0,1:T(8,128)} %fusion.26) | copy-start | bytes 3145732
  277.4 6.6 %copy-start.43 = (s32[80]{0:T(128)S(1)}, s32[80]{0:T(128)}, u32[]{:S(2)}) copy-start(s32[80]{0:T(128)} %subtract_bitcast_fusion.1) | copy-start | bytes 964
  293.3 1.6 copy-start.3
  293.3 1.6 copy-start.24
  296.3 3.0 copy-start.8
  296.3 3.0 copy-start.25
  296.3 3.0 copy-start.38
  303.5 3.6 copy-start.36
  307.0 3.9 copy-start.47
  307.0 9.5 %copy-start.10 = (bf16[4,64,1024]{2,1,0:T(8,128)(2,1)S(1)}, bf16[4,64,1024]{2,1,0:T(8,128)(2,1)}, u32[]{:S(2)}) copy-start(bf16[4,64,1024]{2,1,0:T(8,128)(2,1)} %copy-done.9) | copy-start | bytes 1572868
  310.2 67.8 %copy-start.22 = (bf16[3,64,64]{2,1,0:T(8,128)(2,1)S(1)}, bf16[3,64,64]{2,1,0:T(8,128)(2,1)}, u32[]{:S(2)}) copy-start(bf16[3,64,64]{2,1,0:T(8,128)(2,1)} %param.32) | copy-start | bytes 73732
  310.2 67.8 %copy-start.48 = (f32[64]{0:T(128)S(1)}, f32[64]{0:T(128)}, u32[]{:S(2)}) copy-start(f32[64]{0:T(128)} %get-tuple-element.21) | copy-start | bytes 772
  316.8 61.6 %collective-permute-start.5 = (bf16[256,1024]{0,1:T(8,128)(2,1)S(1)}, bf16[256,1024]{0,1:T(8,128)(2,1)S(1)}, u32[]{:S(2)}, u32[]{:S(2)}) collective-permute-start(bf16[256,1024]{0,1:T(8,128)(2,1)S(1)} %copy.198), channel_id=1, source_target_pairs={{4,0},{8,4},{12,8},{16,12},{20,16},{24,20},{28,24},{5,1},{9,5},{13... | collective-permute-start | bytes 1572872 | tf_op jit(solution)/shard_map/ppermute | solution.py:20
  318.1 61.4 %collective-permute-start.4 = (bf16[256,1024]{0,1:T(8,128)(2,1)S(1)}, bf16[256,1024]{0,1:T(8,128)(2,1)S(1)}, u32[]{:S(2)}, u32[]{:S(2)}) collective-permute-start(bf16[256,1024]{0,1:T(8,128)(2,1)S(1)} %copy.198), channel_id=1, source_target_pairs={{0,4},{4,8},{8,12},{12,16},{16,20},{20,24},{24,28},{1,5},{5,9},{9,... | collective-permute-start | bytes 1572872 | tf_op jit(solution)/shard_map/ppermute | solution.py:18
  387.6 6.6 %copy-start.15 = (f32[8,256,128]{2,0,1:T(8,128)S(1)}, f32[8,256,128]{2,0,1:T(8,128)}, u32[]{:S(2)}) copy-start(f32[8,256,128]{2,0,1:T(8,128)} %fusion.24) | copy-start | bytes 3145732
  387.6 6.6 %copy-start.44 = (s32[80]{0:T(128)S(1)}, s32[80]{0:T(128)}, u32[]{:S(2)}) copy-start(s32[80]{0:T(128)} %subtract_bitcast_fusion.1) | copy-start | bytes 964
  404.7 6.1 %copy-start.28 = (bf16[128,64]{0,1:T(8,128)(2,1)S(1)}, bf16[128,64]{0,1:T(8,128)(2,1)}, u32[]{:S(2)}) copy-start(bf16[128,64]{0,1:T(8,128)(2,1)} %param.45) | copy-start | bytes 49156
  404.7 6.1 %copy-start.29 = (bf16[16,4,64]{2,0,1:T(8,128)(2,1)S(1)}, bf16[16,4,64]{2,0,1:T(8,128)(2,1)}, u32[]{:S(2)}) copy-start(bf16[16,4,64]{2,0,1:T(8,128)(2,1)} %get-tuple-element.4) | copy-start | bytes 24580
  404.7 6.1 %copy-start.53 = (f32[4,64]{1,0:T(4,128)S(1)}, f32[4,64]{1,0:T(4,128)}, u32[]{:S(2)}) copy-start(f32[4,64]{1,0:T(4,128)} %constant_dynamic-slice_fusion) | copy-start | bytes 3076
  404.7 6.3 %copy-start.51 = (f32[64]{0:T(128)S(1)}, f32[64]{0:T(128)}, u32[]{:S(2)}) copy-start(f32[64]{0:T(128)} %param.47) | copy-start | bytes 772
  407.3 12.3 %all-to-all-start.2 = ((bf16[4,2,32768]{2,1,0:T(2,128)(2,1)}), bf16[4,2,32768]{2,1,0:T(2,128)(2,1)S(1)}, u32[]{:S(2)}, u32[]{:S(2)}) async-start(bf16[4,2,32768]{2,1,0:T(2,128)(2,1)} %reshape.487), calls=%async_computation.4 | async-start | bytes 1048576 | tf_op jit(solution)/shard_map/all_to_all | solution.py:179
  410.8 11.6 %copy-start.1 = (bf16[822,64]{0,1:T(8,128)(2,1)S(1)}, bf16[822,64]{0,1:T(8,128)(2,1)}, u32[]{:S(2)}) copy-start(bf16[822,64]{0,1:T(8,128)(2,1)} %param.30) | copy-start | bytes 315652
  (11 other events, 10.3 us)
Sparse Core Ops, SparseCore 0:
  49.6 62.7 reduce-scatter.3
  157.2 60.8 reduce-scatter.5
  311.0 66.0 reduce-scatter.7
